TPU v7x, 32 devices: a whole 2x2x4 slice. The times are simulated.
32 devices in a mesh: groups: 2 (over x), gx: 4 (over y, core), gy: 4 (over z).
Axes of the slice: x: 2, y: 2, z: 4, core: 2. Of those that a mesh axis runs over, the one named last changes fastest.
Arguments:
- features: bfloat16 [8, 4, 4, 64, 256], P(('groups', 'gx'), 'gy'), parts along dimension 0, may hold values from -6 to 6
- neighbour_table: int32 [8, 4, 4, 27], P(('groups', 'gx'), 'gy'), parts along dimension 0, may hold values from 0 to 36, as said below
- kernel_weight: bfloat16 [27, 256, 256], replicated, may hold values from -0.078125 to 0.078125
- out_cotangent: bfloat16 [8, 4, 4, 64, 256], P(('groups', 'gx'), 'gy'), parts along dimension 0, may hold values from -6 to 6
Outputs:
- out_features: bfloat16 [8, 4, 4, 64, 256], P(('groups', 'gx'), 'gy'), parts along dimension 0
- grad_features: bfloat16 [8, 4, 4, 64, 256], P(('groups', 'gx'), 'gy'), parts along dimension 0
- grad_kernel: float32 [13824, 256], P(('groups', 'gx')), parts along dimension 0
There are 2 independent parts, one for each index of `groups`. A program takes and returns all parts, laid end to end along the dimension named above; an argument that names none is the same for every part. Nothing has to cross between parts.
Inputs may be any that keep to these rules, and one draw needn't show every extreme that they name: `neighbour_table`: within a tile the live slots come first; an empty slot has all 27 entries equal to 36; a live slot s has entry 16 + s at offset 13; adjacency is symmetric; some tile has all 4 slots live and the live counts differ much between tiles.
All inputs are finite; a program needn't handle non-finite values.
Results may differ from a plain program's by a relative error of at most 0.001.
Values may be sent and summed in bfloat16 or wider, within the bound.
A program may use at most 128 MiB of HBM per device.

v0:
```python
import jax
import jax.numpy as jnp
from jax import lax
from jax.sharding import PartitionSpec as P

kernel_scale = 0.00390625
offset_list = [
    (first_step, second_step, third_step)
    for first_step in (-1, 0, 1)
    for second_step in (-1, 0, 1)
    for third_step in (-1, 0, 1)
]
source_spans = ((3, 4), (0, 4), (0, 1))


def extended_2(array, sides, width):
    for axis, dim in sides:
        size, length = (lax.axis_size(axis), array.shape[dim])
        up = [(i, (i + 1) % size) for i in range(size - 1)]
        down = [(j, i) for i, j in up]
        last = lax.slice_in_dim(array, length - width, length, axis=dim)
        initial = lax.slice_in_dim(array, 0, width, axis=dim)
        before = lax.ppermute(last, axis, up)
        after = lax.ppermute(initial, axis, down)
        array = jnp.concatenate([before, array, after], axis=dim)
    return array


def assemble_block(extended, brick_table):
    slot_total = brick_table.shape[0]
    channels = extended.shape[-1]
    bricks = extended.reshape(extended.shape[0], 4, 4, 4, channels)
    fetched = jnp.take(bricks, brick_table.reshape(-1), axis=0).reshape(
        slot_total, 27, 4, 4, 4, channels
    )
    planes = []
    for first_step in (-1, 0, 1):
        rows_list = []
        for second_step in (-1, 0, 1):
            pieces = []
            for third_step in (-1, 0, 1):
                offset_index = ((first_step + 1) * 3 + (second_step + 1)) * 3 + (third_step + 1)
                source_x = source_spans[first_step + 1]
                source_y = source_spans[second_step + 1]
                source_z = source_spans[third_step + 1]
                pieces.append(
                    fetched[
                        :,
                        offset_index,
                        source_x[0] : source_x[1],
                        source_y[0] : source_y[1],
                        source_z[0] : source_z[1],
                        :,
                    ]
                )
            rows_list.append(jnp.concatenate(pieces, axis=3))
        planes.append(jnp.concatenate(rows_list, axis=2))
    return jnp.concatenate(planes, axis=1)


def window(padded, shift, sign):
    channels = padded.shape[-1]
    lower = [1 + sign * value for value in shift]
    return padded[
        :, lower[0] : lower[0] + 4, lower[1] : lower[1] + 4, lower[2] : lower[2] + 4, :
    ].reshape(-1, channels)


def forward_conv(padded, kernel_weight):
    summed = None
    for offset_index, shift in enumerate(offset_list):
        product = jnp.dot(
            window(padded, shift, 1),
            kernel_weight[offset_index],
            preferred_element_type=jnp.float32,
        )
        summed = product if summed is None else summed + product
    return summed


def pull_conv(cot_padded, kernel_weight):
    summed = None
    for offset_index, shift in enumerate(offset_list):
        product = lax.dot_general(
            window(cot_padded, shift, -1),
            kernel_weight[offset_index],
            (((1,), (1,)), ((), ())),
            preferred_element_type=jnp.float32,
        )
        summed = product if summed is None else summed + product
    return summed


def kernel_term(padded, cot_flat):
    blocks_list = []
    for offset_index, shift in enumerate(offset_list):
        blocks_list.append(
            lax.dot_general(
                window(padded, shift, 1),
                cot_flat,
                (((0,), (0,)), ((), ())),
                preferred_element_type=jnp.float32,
            )
        )
    return jnp.concatenate(blocks_list, axis=0) * kernel_scale


def widen(beside_all, slot_count, voxels, channels):
    flat = beside_all.reshape(9 * slot_count, voxels, channels)
    return jnp.concatenate([flat, jnp.zeros((1, voxels, channels), beside_all.dtype)], axis=0)


def body(features, neighbour_table, kernel_weight, out_cotangent):
    slot_count = features.shape[2]
    voxels = features.shape[3]
    channels = features.shape[4]
    brick_table = neighbour_table[0, 0]
    beside_all = extended_2(features, (("gx", 0), ("gy", 1)), 1)
    padded = assemble_block(widen(beside_all, slot_count, voxels, channels), brick_table)
    out_flat = forward_conv(padded, kernel_weight).astype(jnp.bfloat16)
    cot_flat = out_cotangent.reshape(slot_count * voxels, channels)
    kernel_part = kernel_term(padded, cot_flat)
    row_part = lax.psum_scatter(kernel_part, "gx", scatter_dimension=0, tiled=True)
    grad_kernel = lax.psum(row_part, "gy")
    cot_around = extended_2(out_cotangent, (("gx", 0), ("gy", 1)), 1)
    cot_padded = assemble_block(widen(cot_around, slot_count, voxels, channels), brick_table)
    grad_flat = pull_conv(cot_padded, kernel_weight).astype(jnp.bfloat16)
    return (out_flat.reshape(features.shape), grad_flat.reshape(features.shape), grad_kernel)


def solution(mesh):
    in_specs = (
        P(("groups", "gx"), "gy", None, None, None),
        P(("groups", "gx"), "gy", None, None),
        P(),
        P(("groups", "gx"), "gy", None, None, None),
    )
    out_specs = (
        P(("groups", "gx"), "gy", None, None, None),
        P(("groups", "gx"), "gy", None, None, None),
        P(("groups", "gx"), None),
    )
    return jax.shard_map(body, mesh=mesh, in_specs=in_specs, out_specs=out_specs, check_vma=False)
```

profile of v0, /device:TPU:0, one launch (start us, length us, event | category | flops | bytes accessed | tf_op | source)
XLA Modules:
  0.0 246.7 jit_solution(3739958742048851636)
XLA Ops:
  7.2 2.4 collective-permute-start
  12.2 5.8 %collective-permute-start.4 = (bf16[1,1,4,64,256]{4,3,2,1,0:T(8,128)(2,1)}, bf16[1,1,4,64,256]{4,3,2,1,0:T(8,128)(2,1)S(1)}, u32[]{:S(2)}, u32[]{:S(2)}) collective-permute-start(bf16[1,1,4,64,256]{4,3,2,1,0:T(8,128)(2,1)} %param.9), channel_id=1, source_target_pairs={{0,4},{4,8},{8,12},{1,5},{5,9},{9,13},{2,6},{6,10},{10,14},{3,7},{... | collective-permute-start | bytes 393224 | tf_op jit(solution)/shard_map/ppermute | solution.py:23
  21.0 4.6 %collective-permute-start.2 = (bf16[3,1,4,64,256]{4,3,2,1,0:T(8,128)(2,1)S(1)}, bf16[3,1,4,64,256]{4,3,2,1,0:T(8,128)(2,1)S(1)}, u32[]{:S(2)}, u32[]{:S(2)}) collective-permute-start(bf16[3,1,4,64,256]{4,3,2,1,0:T(8,128)(2,1)S(1)} %constant_dynamic-update-slice_fusion), channel_id=1, source_target_pairs={{0,1},{1,2},{2,3},{4,5},{5,6},{6,7},{8,9},{9,10},{10,11},{12,13},{... | collective-permute-start | bytes 1179656 | tf_op jit(solution)/shard_map/ppermute | solution.py:23
  27.9 5.3 %collective-permute-start.6 = (bf16[3,1,4,64,256]{4,3,2,1,0:T(8,128)(2,1)S(1)}, bf16[3,1,4,64,256]{4,3,2,1,0:T(8,128)(2,1)}, u32[]{:S(2)}, u32[]{:S(2)}) collective-permute-start(bf16[3,1,4,64,256]{4,3,2,1,0:T(8,128)(2,1)S(1)} %constant_dynamic-update-slice_fusion.3), channel_id=1, source_target_pairs={{0,1},{1,2},{2,3},{4,5},{5,6},{6,7},{8,9},{9,10},{10,11},{12,13},{... | collective-permute-start | bytes 1179656 | tf_op jit(solution)/shard_map/ppermute | solution.py:23
  35.2 6.1 %collective-permute-done.7 = bf16[3,1,4,64,256]{4,3,2,1,0:T(8,128)(2,1)S(1)} collective-permute-done((bf16[3,1,4,64,256]{4,3,2,1,0:T(8,128)(2,1)S(1)}, bf16[3,1,4,64,256]{4,3,2,1,0:T(8,128)(2,1)S(1)}, u32[]{:S(2)}, u32[]{:S(2)}) %collective-permute-start.7) | collective-permute-done | bytes 393248 | tf_op jit(solution)/shard_map/ppermute | solution.py:24
  41.3 1.8 collective-permute-done.6
  45.4 2.5 %reshape.251 = bf16[37,4,4,4,256]{4,3,2,1,0:T(4,128)(2,1)S(1)} reshape(bf16[37,64,256]{2,1,0:T(8,128)(2,1)} %concatenate.194) | data formatting | bytes 2424832 | tf_op jit(solution)/shard_map/reshape | solution.py:32
  47.9 7.1 %gather_fusion.1 = bf16[108,4,4,4,256]{4,3,2,1,0:T(4,128)(2,1)} fusion(bf16[37,4,4,4,256]{4,3,2,1,0:T(4,128)(2,1)S(1)} %reshape.251, s32[1024]{0:T(1024)S(1)} %pad_clamp_fusion), kind=kCustom, calls=%fused_computation.1.clone | custom fusion | bytes 7078320 | tf_op jit(solution)/shard_map/jit(_take)/gather | solution.py:33
  55.0 7.2 %gather_fusion = bf16[108,4,4,4,256]{4,3,2,1,0:T(4,128)(2,1)} fusion(bf16[37,4,4,4,256]{4,3,2,1,0:T(4,128)(2,1)S(1)} %reshape.221, s32[1024]{0:T(1024)S(1)} %pad_clamp_fusion), kind=kCustom, calls=%fused_computation.clone | custom fusion | bytes 7078320 | tf_op jit(solution)/shard_map/jit(_take)/gather | solution.py:33
  62.3 6.4 %broadcast_select_fusion = (bf16[108,4,4,4,256]{4,3,2,1,0:T(4,128)(2,1)S(1)}, bf16[108,4,4,4,256]{4,3,2,1,0:T(4,128)(2,1)S(1)}) fusion(bf16[108,4,4,4,256]{4,3,2,1,0:T(4,128)(2,1)} %gather_fusion.1, pred[108]{0:T(512)(128)(4,1)S(1)} %compare_and_fusion, bf16[108,4,4,4,256]{4,3,2,1,0:T(4,128)(2,1)} %gather_fusion), kind=kLoop, calls=%fused_computation.3 | loop fusion | flops 3538944 | bytes 14155884 | tf_op jit(solution)/shard_map/jit(_take)/select_n | solution.py:33
  90.4 3.3 %broadcast_multiply_fusion = f32[6912,256]{1,0:T(8,128)} fusion(f32[6912,256]{1,0:T(8,128)S(1)} %convolution_dynamic-update-slice_fusion), kind=kLoop, calls=%fused_computation.2 | loop fusion | flops 1769472 | bytes 14155776 | tf_op jit(solution)/shard_map/mul | solution.py:105
  110.2 1.8 reshape.271
  113.5 3.9 %fusion.115 = (bf16[4,4,4,4,256]{4,3,2,1,0:T(4,128)(2,1)}, bf16[4,4,4,4,256]{4,3,2,1,0:T(4,128)(2,1)}, bf16[4,4,4,4,256]{4,3,2,1,0:T(4,128)(2,1)}, bf16[4,4,4,4,...) fusion(bf16[4,5,6,6,256]{4,3,2,1,0:T(8,128)(2,1)} %get-tuple-el, ...), kind=kLoop, calls=%fused_computation.284 | loop fusion | bytes 2359296 | tf_op jit(solution)/shard_map/slice | solution.py:64
  117.4 1.6 reshape.261
  123.8 1.6 reshape.257
  130.2 1.6 reshape.253
  149.3 9.7 %reduce-scatter.2.cloned.1.call-done = f32[1728,256]{1,0:T(8,128)} async-done(((f32[6912,256]{1,0:T(8,128)}), f32[1728,256]{1,0:T(8,128)}) %reduce-scatter.2.cloned.1.call-update) | async-done | bytes 1769488 | tf_op jit(solution)/shard_map/reduce_scatter | solution.py:123
  159.0 1.9 fusion
  165.6 1.6 reshape.275
  167.2 1.6 reshape.274
  168.8 1.6 reshape.273
  170.4 1.6 reshape.272
  179.0 58.1 %all-reduce.4.cloned.1.call-done = f32[1728,256]{1,0:T(8,128)} async-done(((f32[1728,256]{1,0:T(8,128)}), f32[1728,256]{1,0:T(8,128)}) %all-reduce.4.cloned.1.call-update) | async-done | bytes 1769488 | tf_op jit(solution)/shard_map/psum | solution.py:124
  237.1 2.8 %copy.210 = f32[1728,256]{1,0:T(8,128)} copy(f32[1728,256]{1,0:T(8,128)} %all-reduce.4.cloned.1.call-done) | data formatting | bytes 3538944
  (334 shorter events, 88.7 us)
Async XLA Ops:
  7.2 151.8 %reduce-scatter.2.cloned.1.call-start = ((), (), s32[]{:S(2)}) async-start(), calls=%async_computation.1 | async-start | bytes 8847360 | tf_op jit(solution)/shard_map/reduce_scatter | solution.py:123
  7.2 11.6 %collective-permute-start = (bf16[1,1,4,64,256]{4,3,2,1,0:T(8,128)(2,1)}, bf16[1,1,4,64,256]{4,3,2,1,0:T(8,128)(2,1)S(1)}, u32[]{:S(2)}, u32[]{:S(2)}) collective-permute-start(bf16[1,1,4,64,256]{4,3,2,1,0:T(8,128)(2,1)} %param.6), channel_id=1, source_target_pairs={{0,4},{4,8},{8,12},{1,5},{5,9},{9,13},{2,6},{6,10},{10,14},{3,7},{... | collective-permute-start | bytes 393224 | tf_op jit(solution)/shard_map/ppermute | solution.py:23
  9.6 10.1 %collective-permute-start.1 = (bf16[1,1,4,64,256]{4,3,2,1,0:T(8,128)(2,1)}, bf16[1,1,4,64,256]{4,3,2,1,0:T(8,128)(2,1)S(1)}, u32[]{:S(2)}, u32[]{:S(2)}) collective-permute-start(bf16[1,1,4,64,256]{4,3,2,1,0:T(8,128)(2,1)} %param.6), channel_id=1, source_target_pairs={{4,0},{8,4},{12,8},{5,1},{9,5},{13,9},{6,2},{10,6},{14,10},{7,3},{... | collective-permute-start | bytes 393224 | tf_op jit(solution)/shard_map/ppermute | solution.py:24
  10.9 15.7 %collective-permute-start.5 = (bf16[1,1,4,64,256]{4,3,2,1,0:T(8,128)(2,1)}, bf16[1,1,4,64,256]{4,3,2,1,0:T(8,128)(2,1)S(1)}, u32[]{:S(2)}, u32[]{:S(2)}) collective-permute-start(bf16[1,1,4,64,256]{4,3,2,1,0:T(8,128)(2,1)} %param.9), channel_id=1, source_target_pairs={{4,0},{8,4},{12,8},{5,1},{9,5},{13,9},{6,2},{10,6},{14,10},{7,3},{... | collective-permute-start | bytes 393224 | tf_op jit(solution)/shard_map/ppermute | solution.py:24
  12.2 13.4 %collective-permute-start.4 = (bf16[1,1,4,64,256]{4,3,2,1,0:T(8,128)(2,1)}, bf16[1,1,4,64,256]{4,3,2,1,0:T(8,128)(2,1)S(1)}, u32[]{:S(2)}, u32[]{:S(2)}) collective-permute-start(bf16[1,1,4,64,256]{4,3,2,1,0:T(8,128)(2,1)} %param.9), channel_id=1, source_target_pairs={{0,4},{4,8},{8,12},{1,5},{5,9},{9,13},{2,6},{6,10},{10,14},{3,7},{... | collective-permute-start | bytes 393224 | tf_op jit(solution)/shard_map/ppermute | solution.py:23
  19.7 13.5 %collective-permute-start.3 = (bf16[3,1,4,64,256]{4,3,2,1,0:T(8,128)(2,1)S(1)}, bf16[3,1,4,64,256]{4,3,2,1,0:T(8,128)(2,1)S(1)}, u32[]{:S(2)}, u32[]{:S(2)}) collective-permute-start(bf16[3,1,4,64,256]{4,3,2,1,0:T(8,128)(2,1)S(1)} %constant_dynamic-update-slice_fusion), channel_id=1, source_target_pairs={{1,0},{2,1},{3,2},{5,4},{6,5},{7,6},{9,8},{10,9},{11,10},{13,12},{... | collective-permute-start | bytes 1179656 | tf_op jit(solution)/shard_map/ppermute | solution.py:24
  21.0 13.6 %collective-permute-start.2 = (bf16[3,1,4,64,256]{4,3,2,1,0:T(8,128)(2,1)S(1)}, bf16[3,1,4,64,256]{4,3,2,1,0:T(8,128)(2,1)S(1)}, u32[]{:S(2)}, u32[]{:S(2)}) collective-permute-start(bf16[3,1,4,64,256]{4,3,2,1,0:T(8,128)(2,1)S(1)} %constant_dynamic-update-slice_fusion), channel_id=1, source_target_pairs={{0,1},{1,2},{2,3},{4,5},{5,6},{6,7},{8,9},{9,10},{10,11},{12,13},{... | collective-permute-start | bytes 1179656 | tf_op jit(solution)/shard_map/ppermute | solution.py:23
  26.6 14.7 %collective-permute-start.7 = (bf16[3,1,4,64,256]{4,3,2,1,0:T(8,128)(2,1)S(1)}, bf16[3,1,4,64,256]{4,3,2,1,0:T(8,128)(2,1)S(1)}, u32[]{:S(2)}, u32[]{:S(2)}) collective-permute-start(bf16[3,1,4,64,256]{4,3,2,1,0:T(8,128)(2,1)S(1)} %constant_dynamic-update-slice_fusion.3), channel_id=1, source_target_pairs={{1,0},{2,1},{3,2},{5,4},{6,5},{7,6},{9,8},{10,9},{11,10},{13,12},{... | collective-permute-start | bytes 1179656 | tf_op jit(solution)/shard_map/ppermute | solution.py:24
  27.9 15.2 %collective-permute-start.6 = (bf16[3,1,4,64,256]{4,3,2,1,0:T(8,128)(2,1)S(1)}, bf16[3,1,4,64,256]{4,3,2,1,0:T(8,128)(2,1)}, u32[]{:S(2)}, u32[]{:S(2)}) collective-permute-start(bf16[3,1,4,64,256]{4,3,2,1,0:T(8,128)(2,1)S(1)} %constant_dynamic-update-slice_fusion.3), channel_id=1, source_target_pairs={{0,1},{1,2},{2,3},{4,5},{5,6},{6,7},{8,9},{9,10},{10,11},{12,13},{... | collective-permute-start | bytes 1179656 | tf_op jit(solution)/shard_map/ppermute | solution.py:23
  71.3 15.8 %copy-start.4 = (bf16[256,256]{1,0:T(8,128)(2,1)}, bf16[256,256]{1,0:T(8,128)(2,1)S(1)}, u32[]{:S(2)}) copy-start(bf16[256,256]{1,0:T(8,128)(2,1)S(1)} %reshape_squeeze.12) | copy-start | bytes 393220
  71.6 15.7 %copy-start.6 = (bf16[256,256]{1,0:T(8,128)(2,1)}, bf16[256,256]{1,0:T(8,128)(2,1)S(1)}, u32[]{:S(2)}) copy-start(bf16[256,256]{1,0:T(8,128)(2,1)S(1)} %reshape.236) | copy-start | bytes 393220
  71.7 15.2 %copy-start.8 = (bf16[256,256]{1,0:T(8,128)(2,1)}, bf16[256,256]{1,0:T(8,128)(2,1)S(1)}, u32[]{:S(2)}) copy-start(bf16[256,256]{1,0:T(8,128)(2,1)S(1)} %reshape.235) | copy-start | bytes 393220
  73.1 15.0 %copy-start.10 = (bf16[256,256]{1,0:T(8,128)(2,1)}, bf16[256,256]{1,0:T(8,128)(2,1)S(1)}, u32[]{:S(2)}) copy-start(bf16[256,256]{1,0:T(8,128)(2,1)S(1)} %reshape.239) | copy-start | bytes 393220
  73.1 14.7 %copy-start.12 = (bf16[256,256]{1,0:T(8,128)(2,1)}, bf16[256,256]{1,0:T(8,128)(2,1)S(1)}, u32[]{:S(2)}) copy-start(bf16[256,256]{1,0:T(8,128)(2,1)S(1)} %reshape.238) | copy-start | bytes 393220
  73.2 14.4 %copy-start.14 = (bf16[256,256]{1,0:T(8,128)(2,1)}, bf16[256,256]{1,0:T(8,128)(2,1)S(1)}, u32[]{:S(2)}) copy-start(bf16[256,256]{1,0:T(8,128)(2,1)S(1)} %reshape.237) | copy-start | bytes 393220
  73.2 13.0 %copy-start.20 = (bf16[256,256]{1,0:T(8,128)(2,1)}, bf16[256,256]{1,0:T(8,128)(2,1)S(1)}, u32[]{:S(2)}) copy-start(bf16[256,256]{1,0:T(8,128)(2,1)S(1)} %reshape.232) | copy-start | bytes 393220
  73.3 13.1 %copy-start.16 = (bf16[256,256]{1,0:T(8,128)(2,1)}, bf16[256,256]{1,0:T(8,128)(2,1)S(1)}, u32[]{:S(2)}) copy-start(bf16[256,256]{1,0:T(8,128)(2,1)S(1)} %reshape.233) | copy-start | bytes 393220
  73.3 13.3 %copy-start.18 = (bf16[256,256]{1,0:T(8,128)(2,1)}, bf16[256,256]{1,0:T(8,128)(2,1)S(1)}, u32[]{:S(2)}) copy-start(bf16[256,256]{1,0:T(8,128)(2,1)S(1)} %reshape.234) | copy-start | bytes 393220
  74.4 11.6 %copy-start.30 = (bf16[256,256]{1,0:T(8,128)(2,1)}, bf16[256,256]{1,0:T(8,128)(2,1)S(1)}, u32[]{:S(2)}) copy-start(bf16[256,256]{1,0:T(8,128)(2,1)S(1)} %reshape.231) | copy-start | bytes 393220
  74.5 11.3 %copy-start.34 = (bf16[256,256]{1,0:T(8,128)(2,1)}, bf16[256,256]{1,0:T(8,128)(2,1)S(1)}, u32[]{:S(2)}) copy-start(bf16[256,256]{1,0:T(8,128)(2,1)S(1)} %reshape.230) | copy-start | bytes 393220
  74.5 11.0 %copy-start.38 = (bf16[256,256]{1,0:T(8,128)(2,1)}, bf16[256,256]{1,0:T(8,128)(2,1)S(1)}, u32[]{:S(2)}) copy-start(bf16[256,256]{1,0:T(8,128)(2,1)S(1)} %reshape.229) | copy-start | bytes 393220
  78.1 12.1 %copy-start.3 = (bf16[256,256]{1,0:T(8,128)(2,1)}, bf16[256,256]{1,0:T(8,128)(2,1)S(1)}, u32[]{:S(2)}) copy-start(bf16[256,256]{1,0:T(8,128)(2,1)S(1)} %reshape.248) | copy-start | bytes 393220
  93.8 143.2 %all-reduce.4.cloned.1.call-start = ((), (), s32[]{:S(2)}) async-start(), calls=%async_computation.2 | async-start | bytes 3538944 | tf_op jit(solution)/shard_map/psum | solution.py:124
  108.7 23.1 %copy-start.1 = (bf16[27,256,256]{2,1,0:T(8,128)(2,1)S(1)}, bf16[27,256,256]{2,1,0:T(8,128)(2,1)}, u32[]{:S(2)}) copy-start(bf16[27,256,256]{2,1,0:T(8,128)(2,1)} %param.8) | copy-start | bytes 10616836
  (58 other events, 249.1 us)
Sparse Core Ops, SparseCore 0:
  93.9 65.0 reduce-scatter.1
  161.5 75.4 all-reduce.3
where the time goes:
time: 248 us; the launch traced here: 247 us
  local copies, waits for them, and re-layouts  81.1 us (33%)
  waiting for transfers between devices  77.2 us (31%)
  matrix products  33.8 us (14%)
  starting transfers between devices  23.5 us (9%)
  between operations  16.1 us (6%)
  other arithmetic  15 us (6%)
    psum x1, waiting for transfers between devices, body(): grad_kernel = lax.psum(row_part, 'gy')  58.1 us
    reshape x52, local copies, waits for them, and re-layouts, window(): return padded[:, lower[0]:lower[0] + 4, lower[1]:lower[1] + 4, lower[2]:l...  40.1 us
    ppermute x4, starting transfers between devices, extended_2(): before = lax.ppermute(last, axis, up)  18 us
    gather x2, local copies, waits for them, and re-layouts, assemble_block(): jnp.take(bricks, brick_table.reshape(-1), axis=0)  14.4 us
    dot_general x27, matrix products, pull_conv(): lax.dot_general(window(cot_padded, shift, -1), kernel_weight[offset_index...  13 us
    dot_general x27, matrix products, forward_conv(): jnp.dot(window(padded, shift, 1), kernel_weight[offset_index], preferred_...  12.2 us
    reduce_scatter x1, waiting for transfers between devices, body(): lax.psum_scatter(kernel_part, 'gx', scatter_dimension=0, tiled=True)  9.7 us
    dot_general x27, matrix products, kernel_term(): lax.dot_general(window(padded, shift, 1), cot_flat, (((0,), (0,)), ((), (...  8.65 us
  transfers between devices with their start and end apart: 10, of which 5 were waited for; matrix products, arithmetic and copies ran while one was open for 31% of the time, Pallas kernels for 0%

commit v1 on v0

--- a/solution.py
+++ b/solution.py
@@ -121,7 +121,7 @@
     cot_flat = out_cotangent.reshape(slot_count * voxels, channels)
     kernel_part = kernel_term(padded, cot_flat)
     row_part = lax.psum_scatter(kernel_part, "gx", scatter_dimension=0, tiled=True)
-    grad_kernel = lax.psum(row_part, "gy")
+    grad_kernel = lax.all_gather(row_part, "gy").sum(axis=0)
     cot_around = extended_2(out_cotangent, (("gx", 0), ("gy", 1)), 1)
     cot_padded = assemble_block(widen(cot_around, slot_count, voxels, channels), brick_table)
     grad_flat = pull_conv(cot_padded, kernel_weight).astype(jnp.bfloat16)

time: 248 us -> 300 us (1.21)
  waiting for transfers between devices: 77.2 us -> 130 us
  other arithmetic: 15 us -> 21.7 us
  local copies, waits for them, and re-layouts: 81.1 us -> 77.1 us
  matrix products: 33.8 us -> 30.3 us
    all_gather x0 -> x1, waiting for transfers between devices: none -> 114 us  [body(): grad_kernel = lax.all_gather(row_part, 'gy').sum(axis=0)]
    psum x1 -> x0, waiting for transfers between devices: 58.1 us -> none  [body(): grad_kernel = lax.psum(row_part, 'gy')]
    dot_general x27, matrix products: 13 us -> 7.59 us  [pull_conv(): lax.dot_general(window(cot_padded, shift, -1), kernel_weight[offset_index...]
    reduce_sum x0 -> x1, other arithmetic: none -> 4.91 us  [body(): grad_kernel = lax.all_gather(row_part, 'gy').sum(axis=0)]
    unnamed x149 -> x146, local copies, waits for them, and re-layouts: 5.58 us -> 2.15 us
  transfers between devices with their start and end apart: 10 -> 10, of which waited for: 5 -> 5; matrix products, arithmetic and copies ran while one was open for 31% -> 25% of each run, Pallas kernels for 0% -> 0%
where the time goes in v1:
time: 300 us; the launch traced here: 299 us
  waiting for transfers between devices  130 us (43%)
  local copies, waits for them, and re-layouts  77.1 us (26%)
  matrix products  30.3 us (10%)
  starting transfers between devices  23.5 us (8%)
  other arithmetic  21.7 us (7%)
  between operations  16.1 us (5%)
    all_gather x1, waiting for transfers between devices, body(): grad_kernel = lax.all_gather(row_part, 'gy').sum(axis=0)  114 us
    reshape x52, local copies, waits for them, and re-layouts, window(): return padded[:, lower[0]:lower[0] + 4, lower[1]:lower[1] + 4, lower[2]:l...  39.5 us
    ppermute x4, starting transfers between devices, extended_2(): before = lax.ppermute(last, axis, up)  18 us
    dot_general x27, matrix products, forward_conv(): jnp.dot(window(padded, shift, 1), kernel_weight[offset_index], preferred_...  14.9 us
    gather x2, local copies, waits for them, and re-layouts, assemble_block(): jnp.take(bricks, brick_table.reshape(-1), axis=0)  14.2 us
    select_n x2, other arithmetic, assemble_block(): jnp.take(bricks, brick_table.reshape(-1), axis=0)  8.19 us
    slice x6, local copies, waits for them, and re-layouts, window(): padded[:, lower[0]:lower[0] + 4, lower[1]:lower[1] + 4, lower[2]:lower[2]...  7.99 us
    dot_general x27, matrix products, kernel_term(): lax.dot_general(window(padded, shift, 1), cot_flat, (((0,), (0,)), ((), (...  7.75 us
  transfers between devices with their start and end apart: 10, of which 5 were waited for; matrix products, arithmetic and copies ran while one was open for 25% of the time, Pallas kernels for 0%

profile of v1, /device:TPU:0, one launch (start us, length us, event | category | flops | bytes accessed | tf_op | source)
XLA Modules:
  0.0 298.7 jit_solution(11273732983484029783)
XLA Ops:
  7.2 2.4 collective-permute-start
  12.2 5.8 %collective-permute-start.4 = (bf16[1,1,4,64,256]{4,3,2,1,0:T(8,128)(2,1)}, bf16[1,1,4,64,256]{4,3,2,1,0:T(8,128)(2,1)S(1)}, u32[]{:S(2)}, u32[]{:S(2)}) collective-permute-start(bf16[1,1,4,64,256]{4,3,2,1,0:T(8,128)(2,1)} %param.9), channel_id=1, source_target_pairs={{0,4},{4,8},{8,12},{1,5},{5,9},{9,13},{2,6},{6,10},{10,14},{3,7},{... | collective-permute-start | bytes 393224 | tf_op jit(solution)/shard_map/ppermute | solution.py:23
  21.0 4.6 %collective-permute-start.2 = (bf16[3,1,4,64,256]{4,3,2,1,0:T(8,128)(2,1)S(1)}, bf16[3,1,4,64,256]{4,3,2,1,0:T(8,128)(2,1)S(1)}, u32[]{:S(2)}, u32[]{:S(2)}) collective-permute-start(bf16[3,1,4,64,256]{4,3,2,1,0:T(8,128)(2,1)S(1)} %constant_dynamic-update-slice_fusion), channel_id=1, source_target_pairs={{0,1},{1,2},{2,3},{4,5},{5,6},{6,7},{8,9},{9,10},{10,11},{12,13},{... | collective-permute-start | bytes 1179656 | tf_op jit(solution)/shard_map/ppermute | solution.py:23
  27.9 5.3 %collective-permute-start.6 = (bf16[3,1,4,64,256]{4,3,2,1,0:T(8,128)(2,1)S(1)}, bf16[3,1,4,64,256]{4,3,2,1,0:T(8,128)(2,1)}, u32[]{:S(2)}, u32[]{:S(2)}) collective-permute-start(bf16[3,1,4,64,256]{4,3,2,1,0:T(8,128)(2,1)S(1)} %constant_dynamic-update-slice_fusion.3), channel_id=1, source_target_pairs={{0,1},{1,2},{2,3},{4,5},{5,6},{6,7},{8,9},{9,10},{10,11},{12,13},{... | collective-permute-start | bytes 1179656 | tf_op jit(solution)/shard_map/ppermute | solution.py:23
  35.2 6.1 %collective-permute-done.7 = bf16[3,1,4,64,256]{4,3,2,1,0:T(8,128)(2,1)S(1)} collective-permute-done((bf16[3,1,4,64,256]{4,3,2,1,0:T(8,128)(2,1)S(1)}, bf16[3,1,4,64,256]{4,3,2,1,0:T(8,128)(2,1)S(1)}, u32[]{:S(2)}, u32[]{:S(2)}) %collective-permute-start.7) | collective-permute-done | bytes 393248 | tf_op jit(solution)/shard_map/ppermute | solution.py:24
  41.3 1.8 collective-permute-done.6
  45.4 2.5 reshape.251
  47.9 7.1 %gather_fusion.1 = bf16[108,4,4,4,256]{4,3,2,1,0:T(4,128)(2,1)} fusion(bf16[37,4,4,4,256]{4,3,2,1,0:T(4,128)(2,1)S(1)} %reshape.251, s32[1024]{0:T(1024)S(1)} %pad_clamp_fusion), kind=kCustom, calls=%fused_computation.1.clone | custom fusion | bytes 7078320 | tf_op jit(solution)/shard_map/jit(_take)/gather | solution.py:33
  55.0 7.1 %gather_fusion = bf16[108,4,4,4,256]{4,3,2,1,0:T(4,128)(2,1)} fusion(bf16[37,4,4,4,256]{4,3,2,1,0:T(4,128)(2,1)S(1)} %reshape.221, s32[1024]{0:T(1024)S(1)} %pad_clamp_fusion), kind=kCustom, calls=%fused_computation.clone | custom fusion | bytes 7078320 | tf_op jit(solution)/shard_map/jit(_take)/gather | solution.py:33
  62.2 8.2 %broadcast_select_fusion = (bf16[108,4,4,4,256]{4,3,2,1,0:T(4,128)(2,1)}, bf16[108,4,4,4,256]{4,3,2,1,0:T(4,128)(2,1)S(1)}) fusion(bf16[108,4,4,4,256]{4,3,2,1,0:T(4,128)(2,1)} %gather_fusion.1, pred[108]{0:T(512)(128)(4,1)S(1)} %compare_and_fusion, bf16[108,4,4,4,256]{4,3,2,1,0:T(4,128)(2,1)} %gather_fusion), kind=kLoop, calls=%fused_computation.3 | loop fusion | flops 3538944 | bytes 14155884 | tf_op jit(solution)/shard_map/jit(_take)/select_n | solution.py:33
  88.5 3.4 %broadcast_multiply_fusion = f32[6912,256]{1,0:T(8,128)} fusion(f32[6912,256]{1,0:T(8,128)S(1)} %convolution_dynamic-update-slice_fusion), kind=kLoop, calls=%fused_computation.2 | loop fusion | flops 1769472 | bytes 14155776 | tf_op jit(solution)/shard_map/mul | solution.py:105
  109.8 1.8 reshape.278
  111.5 1.6 reshape.277
  113.1 1.6 reshape.276
  114.7 1.7 reshape.275
  116.4 1.6 reshape.274
  118.0 1.6 reshape.273
  119.6 1.6 reshape.272
  124.4 3.9 %fusion.115 = (bf16[4,4,4,4,256]{4,3,2,1,0:T(4,128)(2,1)}, bf16[4,4,4,4,256]{4,3,2,1,0:T(4,128)(2,1)}, bf16[4,4,4,4,256]{4,3,2,1,0:T(4,128)(2,1)}, bf16[4,4,4,4,...) fusion(bf16[4,5,6,6,256]{4,3,2,1,0:T(8,128)(2,1)} %get-tuple-el, ...), kind=kLoop, calls=%fused_computation.284 | loop fusion | bytes 2359296 | tf_op jit(solution)/shard_map/slice | solution.py:64
  128.2 1.6 reshape.261
  137.8 1.6 reshape.255
  149.9 7.1 %reduce-scatter.2.cloned.1.call-done = f32[1728,256]{1,0:T(8,128)} async-done(((f32[6912,256]{1,0:T(8,128)}), f32[1728,256]{1,0:T(8,128)}) %reduce-scatter.2.cloned.1.call-update) | async-done | bytes 1769488 | tf_op jit(solution)/shard_map/reduce_scatter | solution.py:123
  173.5 113.5 %all-gather.3.cloned.1.call-done = f32[6912,256]{1,0:T(8,128)} async-done(((f32[1728,256]{1,0:T(8,128)}), f32[6912,256]{1,0:T(8,128)}) %all-gather.3.cloned.1.call-update) | async-done | bytes 7077904 | tf_op jit(solution)/shard_map/all_gather | solution.py:124
  287.0 4.9 %reduce_sum.9 = f32[1728,256]{1,0:T(8,128)} reduce(f32[4,1728,256]{2,1,0:T(8,128)} %bitcast.424, f32[]{:T(128)} %constant.2.clone.1), dimensions={0}, to_apply=%region_1.3 | reduce | flops 1327104 | bytes 8847364 | tf_op jit(solution)/shard_map/reduce_sum | solution.py:124
  (332 shorter events, 84.4 us)
Async XLA Ops:
  7.2 149.9 %reduce-scatter.2.cloned.1.call-start = ((), (), s32[]{:S(2)}) async-start(), calls=%async_computation.1 | async-start | bytes 8847360 | tf_op jit(solution)/shard_map/reduce_scatter | solution.py:123
  7.2 11.6 %collective-permute-start = (bf16[1,1,4,64,256]{4,3,2,1,0:T(8,128)(2,1)}, bf16[1,1,4,64,256]{4,3,2,1,0:T(8,128)(2,1)S(1)}, u32[]{:S(2)}, u32[]{:S(2)}) collective-permute-start(bf16[1,1,4,64,256]{4,3,2,1,0:T(8,128)(2,1)} %param.6), channel_id=1, source_target_pairs={{0,4},{4,8},{8,12},{1,5},{5,9},{9,13},{2,6},{6,10},{10,14},{3,7},{... | collective-permute-start | bytes 393224 | tf_op jit(solution)/shard_map/ppermute | solution.py:23
  9.6 10.1 %collective-permute-start.1 = (bf16[1,1,4,64,256]{4,3,2,1,0:T(8,128)(2,1)}, bf16[1,1,4,64,256]{4,3,2,1,0:T(8,128)(2,1)S(1)}, u32[]{:S(2)}, u32[]{:S(2)}) collective-permute-start(bf16[1,1,4,64,256]{4,3,2,1,0:T(8,128)(2,1)} %param.6), channel_id=1, source_target_pairs={{4,0},{8,4},{12,8},{5,1},{9,5},{13,9},{6,2},{10,6},{14,10},{7,3},{... | collective-permute-start | bytes 393224 | tf_op jit(solution)/shard_map/ppermute | solution.py:24
  10.9 15.7 %collective-permute-start.5 = (bf16[1,1,4,64,256]{4,3,2,1,0:T(8,128)(2,1)}, bf16[1,1,4,64,256]{4,3,2,1,0:T(8,128)(2,1)S(1)}, u32[]{:S(2)}, u32[]{:S(2)}) collective-permute-start(bf16[1,1,4,64,256]{4,3,2,1,0:T(8,128)(2,1)} %param.9), channel_id=1, source_target_pairs={{4,0},{8,4},{12,8},{5,1},{9,5},{13,9},{6,2},{10,6},{14,10},{7,3},{... | collective-permute-start | bytes 393224 | tf_op jit(solution)/shard_map/ppermute | solution.py:24
  12.2 13.4 %collective-permute-start.4 = (bf16[1,1,4,64,256]{4,3,2,1,0:T(8,128)(2,1)}, bf16[1,1,4,64,256]{4,3,2,1,0:T(8,128)(2,1)S(1)}, u32[]{:S(2)}, u32[]{:S(2)}) collective-permute-start(bf16[1,1,4,64,256]{4,3,2,1,0:T(8,128)(2,1)} %param.9), channel_id=1, source_target_pairs={{0,4},{4,8},{8,12},{1,5},{5,9},{9,13},{2,6},{6,10},{10,14},{3,7},{... | collective-permute-start | bytes 393224 | tf_op jit(solution)/shard_map/ppermute | solution.py:23
  19.7 13.5 %collective-permute-start.3 = (bf16[3,1,4,64,256]{4,3,2,1,0:T(8,128)(2,1)S(1)}, bf16[3,1,4,64,256]{4,3,2,1,0:T(8,128)(2,1)S(1)}, u32[]{:S(2)}, u32[]{:S(2)}) collective-permute-start(bf16[3,1,4,64,256]{4,3,2,1,0:T(8,128)(2,1)S(1)} %constant_dynamic-update-slice_fusion), channel_id=1, source_target_pairs={{1,0},{2,1},{3,2},{5,4},{6,5},{7,6},{9,8},{10,9},{11,10},{13,12},{... | collective-permute-start | bytes 1179656 | tf_op jit(solution)/shard_map/ppermute | solution.py:24
  21.0 13.6 %collective-permute-start.2 = (bf16[3,1,4,64,256]{4,3,2,1,0:T(8,128)(2,1)S(1)}, bf16[3,1,4,64,256]{4,3,2,1,0:T(8,128)(2,1)S(1)}, u32[]{:S(2)}, u32[]{:S(2)}) collective-permute-start(bf16[3,1,4,64,256]{4,3,2,1,0:T(8,128)(2,1)S(1)} %constant_dynamic-update-slice_fusion), channel_id=1, source_target_pairs={{0,1},{1,2},{2,3},{4,5},{5,6},{6,7},{8,9},{9,10},{10,11},{12,13},{... | collective-permute-start | bytes 1179656 | tf_op jit(solution)/shard_map/ppermute | solution.py:23
  26.6 14.7 %collective-permute-start.7 = (bf16[3,1,4,64,256]{4,3,2,1,0:T(8,128)(2,1)S(1)}, bf16[3,1,4,64,256]{4,3,2,1,0:T(8,128)(2,1)S(1)}, u32[]{:S(2)}, u32[]{:S(2)}) collective-permute-start(bf16[3,1,4,64,256]{4,3,2,1,0:T(8,128)(2,1)S(1)} %constant_dynamic-update-slice_fusion.3), channel_id=1, source_target_pairs={{1,0},{2,1},{3,2},{5,4},{6,5},{7,6},{9,8},{10,9},{11,10},{13,12},{... | collective-permute-start | bytes 1179656 | tf_op jit(solution)/shard_map/ppermute | solution.py:24
  27.9 15.2 %collective-permute-start.6 = (bf16[3,1,4,64,256]{4,3,2,1,0:T(8,128)(2,1)S(1)}, bf16[3,1,4,64,256]{4,3,2,1,0:T(8,128)(2,1)}, u32[]{:S(2)}, u32[]{:S(2)}) collective-permute-start(bf16[3,1,4,64,256]{4,3,2,1,0:T(8,128)(2,1)S(1)} %constant_dynamic-update-slice_fusion.3), channel_id=1, source_target_pairs={{0,1},{1,2},{2,3},{4,5},{5,6},{6,7},{8,9},{9,10},{10,11},{12,13},{... | collective-permute-start | bytes 1179656 | tf_op jit(solution)/shard_map/ppermute | solution.py:23
  70.9 14.3 %copy-start.4 = (bf16[256,256]{1,0:T(8,128)(2,1)}, bf16[256,256]{1,0:T(8,128)(2,1)S(1)}, u32[]{:S(2)}) copy-start(bf16[256,256]{1,0:T(8,128)(2,1)S(1)} %reshape_squeeze.12) | copy-start | bytes 393220
  71.2 14.2 %copy-start.5 = (bf16[256,256]{1,0:T(8,128)(2,1)}, bf16[256,256]{1,0:T(8,128)(2,1)S(1)}, u32[]{:S(2)}) copy-start(bf16[256,256]{1,0:T(8,128)(2,1)S(1)} %reshape.236) | copy-start | bytes 393220
  71.3 13.7 %copy-start.7 = (bf16[256,256]{1,0:T(8,128)(2,1)}, bf16[256,256]{1,0:T(8,128)(2,1)S(1)}, u32[]{:S(2)}) copy-start(bf16[256,256]{1,0:T(8,128)(2,1)S(1)} %reshape.235) | copy-start | bytes 393220
  72.7 13.5 %copy-start.8 = (bf16[256,256]{1,0:T(8,128)(2,1)}, bf16[256,256]{1,0:T(8,128)(2,1)S(1)}, u32[]{:S(2)}) copy-start(bf16[256,256]{1,0:T(8,128)(2,1)S(1)} %reshape.239) | copy-start | bytes 393220
  72.7 13.2 %copy-start.10 = (bf16[256,256]{1,0:T(8,128)(2,1)}, bf16[256,256]{1,0:T(8,128)(2,1)S(1)}, u32[]{:S(2)}) copy-start(bf16[256,256]{1,0:T(8,128)(2,1)S(1)} %reshape.238) | copy-start | bytes 393220
  72.8 12.9 %copy-start.12 = (bf16[256,256]{1,0:T(8,128)(2,1)}, bf16[256,256]{1,0:T(8,128)(2,1)S(1)}, u32[]{:S(2)}) copy-start(bf16[256,256]{1,0:T(8,128)(2,1)S(1)} %reshape.237) | copy-start | bytes 393220
  72.8 11.4 %copy-start.16 = (bf16[256,256]{1,0:T(8,128)(2,1)}, bf16[256,256]{1,0:T(8,128)(2,1)S(1)}, u32[]{:S(2)}) copy-start(bf16[256,256]{1,0:T(8,128)(2,1)S(1)} %reshape.232) | copy-start | bytes 393220
  72.9 11.6 %copy-start.14 = (bf16[256,256]{1,0:T(8,128)(2,1)}, bf16[256,256]{1,0:T(8,128)(2,1)S(1)}, u32[]{:S(2)}) copy-start(bf16[256,256]{1,0:T(8,128)(2,1)S(1)} %reshape.233) | copy-start | bytes 393220
  72.9 11.8 %copy-start.15 = (bf16[256,256]{1,0:T(8,128)(2,1)}, bf16[256,256]{1,0:T(8,128)(2,1)S(1)}, u32[]{:S(2)}) copy-start(bf16[256,256]{1,0:T(8,128)(2,1)S(1)} %reshape.234) | copy-start | bytes 393220
  74.0 10.0 %copy-start.32 = (bf16[256,256]{1,0:T(8,128)(2,1)}, bf16[256,256]{1,0:T(8,128)(2,1)S(1)}, u32[]{:S(2)}) copy-start(bf16[256,256]{1,0:T(8,128)(2,1)S(1)} %reshape.231) | copy-start | bytes 393220
  74.0 9.7 %copy-start.36 = (bf16[256,256]{1,0:T(8,128)(2,1)}, bf16[256,256]{1,0:T(8,128)(2,1)S(1)}, u32[]{:S(2)}) copy-start(bf16[256,256]{1,0:T(8,128)(2,1)S(1)} %reshape.230) | copy-start | bytes 393220
  74.1 9.5 %copy-start.38 = (bf16[256,256]{1,0:T(8,128)(2,1)}, bf16[256,256]{1,0:T(8,128)(2,1)S(1)}, u32[]{:S(2)}) copy-start(bf16[256,256]{1,0:T(8,128)(2,1)S(1)} %reshape.229) | copy-start | bytes 393220
  78.0 10.3 %copy-start.2 = (bf16[256,256]{1,0:T(8,128)(2,1)}, bf16[256,256]{1,0:T(8,128)(2,1)S(1)}, u32[]{:S(2)}) copy-start(bf16[256,256]{1,0:T(8,128)(2,1)S(1)} %reshape.248) | copy-start | bytes 393220
  91.9 195.1 %all-gather.3.cloned.1.call-start = ((), (), s32[]{:S(2)}) async-start(), calls=%async_computation.2 | async-start | bytes 8847360 | tf_op jit(solution)/shard_map/all_gather | solution.py:124
  109.8 32.8 %copy-start.1 = (bf16[27,256,256]{2,1,0:T(8,128)(2,1)S(1)}, bf16[27,256,256]{2,1,0:T(8,128)(2,1)}, u32[]{:S(2)}) copy-start(bf16[27,256,256]{2,1,0:T(8,128)(2,1)} %param.8) | copy-start | bytes 10616836
  (57 other events, 253.7 us)
Sparse Core Ops, SparseCore 0:
  92.0 65.0 reduce-scatter.1
  158.7 128.2 all-gather.2
